TPU v7x, 256 devices: a whole 4x4x8 slice. The times are simulated.
256 devices in a mesh: chan: 32 (over z, y_hi, core), tm: 8 (over y_lo, x).
Axes of the slice: x: 4, y: 4 (y_hi: 2, y_lo: 2; y = y_hi * 2 + y_lo), z: 8, core: 2. Of those that a mesh axis runs over, the one named last changes fastest.
Arguments:
- traces: bfloat16 [32, 192, 128, 1024], P('chan', 'tm'), may hold values from -6 to 6
- valid_mask: int32 [32, 192, 1024], P('chan', 'tm'), may hold values 0 or 1
- pair_owner: int32 [32, 4], P('chan'), may hold values from -1 to 31, as said below
Outputs:
- correlations: float32 [32, 4, 101, 128], P('chan')
Inputs may be any that keep to these rules, and one draw needn't show every extreme that they name: `pair_owner`: row r lists distinct owners in r + 1 .. r + 4 (within the cable) in its leading slots, then -1; every reader with a block above it has one pair or more, and reader 0 fills all 4 slots.
All inputs are finite; a program needn't handle non-finite values. No bound on the sum of `valid_mask` on one device may be relied on, other than what follows from the above.
Results may differ from a plain program's by a relative error of at most 0.0052.
Values may be sent and summed in bfloat16 or wider, within the bound.
No kernel may reach another device: no remote copies, remote signals or barrier semaphores. Data moves between devices by JAX's collectives and lax.ppermute only.
A program may use at most 64 MiB of HBM per device.

v0:
```python
import math
import jax
import jax.numpy as jnp
from jax import lax
from jax.sharding import PartitionSpec as P

NF = 256
MAXLAG = 50
SMOOTH = 4
REACH = 4
water_level = 0.05
eps = 1e-06


def shifted(block, axis, distance):
    devices = range(lax.axis_size(axis))
    route = [(i - distance, i) for i in devices if i - distance in devices]
    return lax.ppermute(block, axis, route)


def forward_table(samples_count, bins_count):
    samples = jnp.arange(samples_count, dtype=jnp.int32)
    bins = jnp.arange(1, bins_count + 1, dtype=jnp.int32)
    phase = samples[:, None] * bins[None, :] % samples_count
    angle = phase.astype(jnp.float32) * jnp.float32(2.0 * math.pi / samples_count)
    return jnp.concatenate([jnp.cos(angle), -jnp.sin(angle)], axis=1).astype(jnp.bfloat16)


def inverse_table(samples_count, bins_count, windows_all):
    bins = jnp.arange(1, bins_count + 1, dtype=jnp.int32)
    offsets = jnp.arange(2 * MAXLAG + 1, dtype=jnp.int32) - MAXLAG
    phase = bins[:, None] * offsets[None, :] % samples_count
    angle = phase.astype(jnp.float32) * jnp.float32(2.0 * math.pi / samples_count)
    factor = jnp.float32(1.0 / math.sqrt(windows_all * bins_count))
    return jnp.concatenate([jnp.cos(angle), -jnp.sin(angle)], axis=0) * factor


def whiten(block_traces, block_mask, forward, bins_count):
    masked = block_traces * block_mask[:, None, :].astype(jnp.bfloat16)
    wins, chans, samples = masked.shape
    spectra = jnp.dot(
        masked.reshape(wins * chans, samples), forward, preferred_element_type=jnp.float32
    )
    spectra = spectra.reshape(wins, chans, 2 * bins_count)
    real_part = spectra[..., :bins_count]
    imag_part = spectra[..., bins_count:]
    amplitude = jnp.sqrt(real_part * real_part + imag_part * imag_part)
    padded = jnp.pad(amplitude, ((0, 0), (0, 0), (SMOOTH, SMOOTH)))
    smooth = padded[..., 0:bins_count]
    for j in range(1, 2 * SMOOTH + 1):
        smooth = smooth + padded[..., j : j + bins_count]
    smooth = smooth / jnp.float32(2 * SMOOTH + 1)
    divisor = smooth + water_level * jnp.mean(amplitude, axis=-1, keepdims=True) + eps
    return (spectra / jnp.concatenate([divisor, divisor], axis=-1)).astype(jnp.bfloat16)


def cross_spectrum(own_spec, other_spec, bins_count):
    swapped = jnp.concatenate([other_spec[..., bins_count:], other_spec[..., :bins_count]], axis=-1)
    direct = jnp.einsum("wcf,wcf->cf", own_spec, other_spec, preferred_element_type=jnp.float32)
    crossed = jnp.einsum("wcf,wcf->cf", own_spec, swapped, preferred_element_type=jnp.float32)
    return jnp.concatenate(
        [
            direct[:, :bins_count] + direct[:, bins_count:],
            crossed[:, :bins_count] - crossed[:, bins_count:],
        ],
        axis=-1,
    )


def body(traces, valid_mask, pair_owner):
    wins_here = traces.shape[1]
    samples_count = traces.shape[3]
    bins_count = NF
    windows_all = wins_here * lax.axis_size("tm")
    forward = forward_table(samples_count, bins_count)
    inverse = inverse_table(samples_count, bins_count, windows_all)
    own_spec = whiten(traces[0], valid_mask[0], forward, bins_count)
    reader = lax.axis_index("chan")
    owners = pair_owner[0]
    chans = own_spec.shape[1]
    stacks = jnp.zeros((REACH, chans, 2 * bins_count), jnp.float32)
    for distance in range(1, REACH + 1):
        arrived = shifted(own_spec, "chan", -distance)
        chosen = (owners == reader + distance).astype(jnp.float32)
        cross = cross_spectrum(own_spec, arrived, bins_count)
        stacks = stacks + chosen[:, None, None] * cross[None, :, :]
    summed = lax.psum(stacks, "tm")
    result = jnp.einsum("pck,kl->plc", summed, inverse, precision=lax.Precision.HIGHEST)
    return result[None]


def solution(mesh):
    return jax.shard_map(
        body,
        mesh=mesh,
        in_specs=(P("chan", "tm", None, None), P("chan", "tm", None), P("chan", None)),
        out_specs=P("chan", None, None, None),
        check_vma=False,
    )
```

profile of v0, /device:TPU:32, one launch (start us, length us, event | category | flops | bytes accessed | tf_op | source)
XLA Modules:
  0.0 380.4 jit_solution(3332210686201202869)
XLA Ops:
  6.5 0.0 all-reduce.3.cloned.1.call-start
  6.5 4.4 %cosine_convert_fusion = (bf16[1024,256]{1,0:T(8,128)(2,1)S(1)}, bf16[1024,256]{1,0:T(8,128)(2,1)S(1)}) fusion(s32[256]{0:T(256)S(1)} %iota_add_fusion), kind=kLoop, calls=%fused_computation.60 | loop fusion | flops 4456448 | bytes 1049600 | tf_op jit(solution)/shard_map/convert.4
  11.0 0.9 convert_bitcast_fusion
  11.9 5.6 %fusion.9 = f32[24,128,512]{2,1,0:T(8,128)S(1)} fusion(bf16[1,24,128,1024]{3,2,1,0:T(8,128)(2,1)} %param.3, bf16[24,1024]{1,0:T(8,128)(2,1)S(1)} %convert_bitcast_fusion, bf16[1024,256]{1,0:T(8,128)(2,1)S(1)} %get-tuple-element.26, bf16[1024,256]{1,0:T(8,128)(2,1)S(1)} %get-tuple-element.25), kind=kOutput, calls=%fused_computation.27 | convolution fusion | flops 3226468352 | bytes 13680640 | tf_op jit(solution)/shard_map/dot_general | solution.py:41
  17.4 1.2 fusion.48
  18.6 8.2 %fusion.20 = f32[24,128,256]{2,1,0:T(8,128)} fusion(f32[24,128,256]{2,1,0:T(8,128)S(1)} %get-tuple-element.14, f32[24,128]{1,0:T(8,128)S(1)} %broadcast_multiply_fusion), kind=kLoop, calls=%fused_computation.38 | loop fusion | flops 8650752 | bytes 6303744 | tf_op jit(solution)/shard_map/add | solution.py:53
  26.9 0.0 copy-start
  26.9 5.0 %fusion.8 = bf16[24,128,512]{2,1,0:T(8,128)(2,1)} fusion(f32[24,128,512]{2,1,0:T(8,128)S(1)} %fusion.9, f32[24,128,256]{2,1,0:T(8,128)} %fusion.20), kind=kLoop, calls=%fused_computation.25 | loop fusion | flops 4718592 | bytes 12582912 | tf_op jit(solution)/shard_map/convert_element_type | solution.py:54
  31.9 4.1 %collective-permute-start = (bf16[24,128,512]{2,1,0:T(8,128)(2,1)}, bf16[24,128,512]{2,1,0:T(8,128)(2,1)S(1)}, u32[]{:S(2)}, u32[]{:S(2)}) collective-permute-start(bf16[24,128,512]{2,1,0:T(8,128)(2,1)} %fusion.8), channel_id=1, source_target_pairs={{8,0},{16,8},{24,16},{32,24},{40,32},{48,40},{56,48},{64,56},{72,6... | collective-permute-start | bytes 9437192 | tf_op jit(solution)/shard_map/ppermute | solution.py:18
  36.0 2.5 collective-permute-start.1
  38.5 1.9 collective-permute-start.2
  40.4 2.1 collective-permute-start.3
  42.5 0.0 copy-done
  42.6 60.2 %collective-permute-done = bf16[24,128,512]{2,1,0:T(8,128)(2,1)S(1)} collective-permute-done((bf16[24,128,512]{2,1,0:T(8,128)(2,1)}, bf16[24,128,512]{2,1,0:T(8,128)(2,1)S(1)}, u32[]{:S(2)}, u32[]{:S(2)}) %collective-permute-start) | collective-permute-done | bytes 3145760 | tf_op jit(solution)/shard_map/ppermute | solution.py:18
  102.8 0.4 fusion.50
  103.2 68.7 %collective-permute-done.1 = bf16[24,128,512]{2,1,0:T(8,128)(2,1)} collective-permute-done((bf16[24,128,512]{2,1,0:T(8,128)(2,1)}, bf16[24,128,512]{2,1,0:T(8,128)(2,1)}, u32[]{:S(2)}, u32[]{:S(2)}) %collective-permute-start.1) | collective-permute-done | bytes 3145760 | tf_op jit(solution)/shard_map/ppermute | solution.py:18
  171.9 2.1 fusion.51
  174.0 63.6 %collective-permute-done.2 = bf16[24,128,512]{2,1,0:T(8,128)(2,1)} collective-permute-done((bf16[24,128,512]{2,1,0:T(8,128)(2,1)}, bf16[24,128,512]{2,1,0:T(8,128)(2,1)}, u32[]{:S(2)}, u32[]{:S(2)}) %collective-permute-start.2) | collective-permute-done | bytes 3145760 | tf_op jit(solution)/shard_map/ppermute | solution.py:18
  237.6 2.1 fusion.52
  239.7 36.0 %collective-permute-done.3 = bf16[24,128,512]{2,1,0:T(8,128)(2,1)} collective-permute-done((bf16[24,128,512]{2,1,0:T(8,128)(2,1)}, bf16[24,128,512]{2,1,0:T(8,128)(2,1)}, u32[]{:S(2)}, u32[]{:S(2)}) %collective-permute-start.3) | collective-permute-done | bytes 3145760 | tf_op jit(solution)/shard_map/ppermute | solution.py:18
  275.7 2.1 fusion.53
  277.8 8.5 %fusion = (f32[128,512]{1,0:T(8,128)S(1)}, f32[128,512]{1,0:T(8,128)S(1)}, f32[128,512]{1,0:T(8,128)S(1)}, f32[128,512]{1,0:T(8,128)S(1)}, f32[128,512]{1,0:T(8,...) fusion(bf16[24,128,512]{2,1,0:T(8,128)(2,1)S(1)} %collective-permute-done, ...), kind=kLoop, calls=%fused_computation.16 | loop fusion | flops 63963136 | bytes 30408704 | tf_op jit(solution)/shard_map/wcf,wcf->cf/dot_general | solution.py:59
  286.5 1.3 multiply_add_fusion
  287.9 0.0 all-reduce.3.cloned.1.call-update
  287.9 0.5 fusion.40
  288.4 82.1 %all-reduce.3.cloned.1.call-done = f32[4,128,512]{2,1,0:T(8,128)} async-done(((f32[4,128,512]{2,1,0:T(8,128)}), f32[4,128,512]{2,1,0:T(8,128)}) %all-reduce.3.cloned.1.call-update) | async-done | bytes 1048592 | tf_op jit(solution)/shard_map/psum | solution.py:87
  370.5 2.3 convolution_bitcast_fusion
  372.8 0.7 copy.4
  (12 shorter events, 0.2 us)
Async XLA Ops:
  6.5 363.9 %all-reduce.3.cloned.1.call-start = ((), (), s32[]{:S(2)}) async-start(), calls=%async_computation | async-start | bytes 2097152 | tf_op jit(solution)/shard_map/psum | solution.py:87
  26.9 15.7 %copy-start = (s32[1,4]{1,0:T(1,128)S(1)}, s32[1,4]{1,0:T(1,128)}, u32[]{:S(2)}) copy-start(s32[1,4]{1,0:T(1,128)} %param.5) | copy-start | bytes 52
  31.9 70.9 %collective-permute-start = (bf16[24,128,512]{2,1,0:T(8,128)(2,1)}, bf16[24,128,512]{2,1,0:T(8,128)(2,1)S(1)}, u32[]{:S(2)}, u32[]{:S(2)}) collective-permute-start(bf16[24,128,512]{2,1,0:T(8,128)(2,1)} %fusion.8), channel_id=1, source_target_pairs={{8,0},{16,8},{24,16},{32,24},{40,32},{48,40},{56,48},{64,56},{72,6... | collective-permute-start | bytes 9437192 | tf_op jit(solution)/shard_map/ppermute | solution.py:18
  36.0 135.9 %collective-permute-start.1 = (bf16[24,128,512]{2,1,0:T(8,128)(2,1)}, bf16[24,128,512]{2,1,0:T(8,128)(2,1)}, u32[]{:S(2)}, u32[]{:S(2)}) collective-permute-start(bf16[24,128,512]{2,1,0:T(8,128)(2,1)} %fusion.8), channel_id=1, source_target_pairs={{16,0},{24,8},{32,16},{40,24},{48,32},{56,40},{64,48},{72,56},{80,... | collective-permute-start | bytes 9437192 | tf_op jit(solution)/shard_map/ppermute | solution.py:18
  38.5 199.1 %collective-permute-start.2 = (bf16[24,128,512]{2,1,0:T(8,128)(2,1)}, bf16[24,128,512]{2,1,0:T(8,128)(2,1)}, u32[]{:S(2)}, u32[]{:S(2)}) collective-permute-start(bf16[24,128,512]{2,1,0:T(8,128)(2,1)} %fusion.8), channel_id=1, source_target_pairs={{24,0},{32,8},{40,16},{48,24},{56,32},{64,40},{72,48},{80,56},{88,... | collective-permute-start | bytes 9437192 | tf_op jit(solution)/shard_map/ppermute | solution.py:18
  40.4 235.3 %collective-permute-start.3 = (bf16[24,128,512]{2,1,0:T(8,128)(2,1)}, bf16[24,128,512]{2,1,0:T(8,128)(2,1)}, u32[]{:S(2)}, u32[]{:S(2)}) collective-permute-start(bf16[24,128,512]{2,1,0:T(8,128)(2,1)} %fusion.8), channel_id=1, source_target_pairs={{32,0},{40,8},{48,16},{56,24},{64,32},{72,40},{80,48},{88,56},{96,... | collective-permute-start | bytes 9437192 | tf_op jit(solution)/shard_map/ppermute | solution.py:18
Sparse Core Ops, SparseCore 0:
  288.0 82.4 all-reduce.2
where the time goes:
time: 381 us; the launch traced here: 380 us
  waiting for transfers between devices  311 us (82%)
  other arithmetic  30.3 us (8%)
  between operations  13.6 us (4%)
  starting transfers between devices  10.6 us (3%)
  matrix products  7.9 us (2%)
  local copies, waits for them, and re-layouts  7.39 us (2%)
    ppermute x4, waiting for transfers between devices, shifted(): return lax.ppermute(block, axis, route)  229 us
    psum x1, waiting for transfers between devices, body(): summed = lax.psum(stacks, 'tm')  82.1 us
    ppermute x4, starting transfers between devices, shifted(): return lax.ppermute(block, axis, route)  10.6 us
    dot_general x1, other arithmetic, cross_spectrum(): jnp.einsum('wcf,wcf->cf', own_spec, other_spec, preferred_element_type=jn...  8.46 us
    add x1, other arithmetic, whiten(): smooth + water_level * jnp.mean(amplitude, axis=-1, keepdims=True) + eps  8.23 us
  transfers between devices with their start and end apart: 5, of which 5 were waited for; matrix products, arithmetic and copies ran while one was open for 1% of the time, Pallas kernels for 0%

commit v1 on v0

--- a/solution.py
+++ b/solution.py
@@ -84,7 +84,7 @@
         chosen = (owners == reader + distance).astype(jnp.float32)
         cross = cross_spectrum(own_spec, arrived, bins_count)
         stacks = stacks + chosen[:, None, None] * cross[None, :, :]
-    summed = lax.psum(stacks, "tm")
+    summed = lax.all_gather(stacks, "tm").sum(axis=0)
     result = jnp.einsum("pck,kl->plc", summed, inverse, precision=lax.Precision.HIGHEST)
     return result[None]
 

time: 381 us -> 397 us (1.042)
  waiting for transfers between devices: 311 us -> 323 us
  other arithmetic: 30.3 us -> 34.9 us
    all_gather x0 -> x1, waiting for transfers between devices: none -> 94.1 us  [body(): summed = lax.all_gather(stacks, 'tm').sum(axis=0)]
    psum x1 -> x0, waiting for transfers between devices: 82.1 us -> none  [body(): summed = lax.psum(stacks, 'tm')]
    reduce_sum x0 -> x1, other arithmetic: none -> 4.54 us  [body(): summed = lax.all_gather(stacks, 'tm').sum(axis=0)]
where the time goes in v1:
time: 397 us; the launch traced here: 396 us
  waiting for transfers between devices  323 us (81%)
  other arithmetic  34.9 us (9%)
  between operations  13.6 us (3%)
  starting transfers between devices  10.6 us (3%)
  local copies, waits for them, and re-layouts  7.39 us (2%)
  matrix products  6.69 us (2%)
    ppermute x4, waiting for transfers between devices, shifted(): return lax.ppermute(block, axis, route)  229 us
    all_gather x1, waiting for transfers between devices, body(): summed = lax.all_gather(stacks, 'tm').sum(axis=0)  94.1 us
    ppermute x4, starting transfers between devices, shifted(): return lax.ppermute(block, axis, route)  10.6 us
    dot_general x1, other arithmetic, cross_spectrum(): jnp.einsum('wcf,wcf->cf', own_spec, other_spec, preferred_element_type=jn...  8.46 us
    add x1, other arithmetic, whiten(): smooth + water_level * jnp.mean(amplitude, axis=-1, keepdims=True) + eps  8.23 us
  transfers between devices with their start and end apart: 5, of which 5 were waited for; matrix products, arithmetic and copies ran while one was open for 1% of the time, Pallas kernels for 0%

profile of v1, /device:TPU:32, one launch (start us, length us, event | category | flops | bytes accessed | tf_op | source)
XLA Modules:
  0.0 395.8 jit_solution(6343607319746294733)
XLA Ops:
  6.5 0.0 all-gather.2.cloned.1.call-start
  6.5 4.4 %cosine_convert_fusion = (bf16[1024,256]{1,0:T(8,128)(2,1)S(1)}, bf16[1024,256]{1,0:T(8,128)(2,1)S(1)}) fusion(s32[256]{0:T(256)S(1)} %iota_add_fusion), kind=kLoop, calls=%fused_computation.60 | loop fusion | flops 4456448 | bytes 1049600 | tf_op jit(solution)/shard_map/convert.4
  11.0 0.9 convert_bitcast_fusion
  11.9 5.6 %fusion.9 = f32[24,128,512]{2,1,0:T(8,128)S(1)} fusion(bf16[1,24,128,1024]{3,2,1,0:T(8,128)(2,1)} %param.3, bf16[24,1024]{1,0:T(8,128)(2,1)S(1)} %convert_bitcast_fusion, bf16[1024,256]{1,0:T(8,128)(2,1)S(1)} %get-tuple-element.26, bf16[1024,256]{1,0:T(8,128)(2,1)S(1)} %get-tuple-element.25), kind=kOutput, calls=%fused_computation.27 | convolution fusion | flops 3226468352 | bytes 13680640 | tf_op jit(solution)/shard_map/dot_general | solution.py:41
  17.4 1.2 fusion.48
  18.6 8.2 %fusion.20 = f32[24,128,256]{2,1,0:T(8,128)} fusion(f32[24,128,256]{2,1,0:T(8,128)S(1)} %get-tuple-element.14, f32[24,128]{1,0:T(8,128)S(1)} %broadcast_multiply_fusion), kind=kLoop, calls=%fused_computation.38 | loop fusion | flops 8650752 | bytes 6303744 | tf_op jit(solution)/shard_map/add | solution.py:53
  26.9 0.0 copy-start
  26.9 5.0 %fusion.8 = bf16[24,128,512]{2,1,0:T(8,128)(2,1)} fusion(f32[24,128,512]{2,1,0:T(8,128)S(1)} %fusion.9, f32[24,128,256]{2,1,0:T(8,128)} %fusion.20), kind=kLoop, calls=%fused_computation.25 | loop fusion | flops 4718592 | bytes 12582912 | tf_op jit(solution)/shard_map/convert_element_type | solution.py:54
  31.9 4.1 %collective-permute-start = (bf16[24,128,512]{2,1,0:T(8,128)(2,1)}, bf16[24,128,512]{2,1,0:T(8,128)(2,1)S(1)}, u32[]{:S(2)}, u32[]{:S(2)}) collective-permute-start(bf16[24,128,512]{2,1,0:T(8,128)(2,1)} %fusion.8), channel_id=1, source_target_pairs={{8,0},{16,8},{24,16},{32,24},{40,32},{48,40},{56,48},{64,56},{72,6... | collective-permute-start | bytes 9437192 | tf_op jit(solution)/shard_map/ppermute | solution.py:18
  36.0 2.5 collective-permute-start.1
  38.5 1.9 collective-permute-start.2
  40.4 2.1 collective-permute-start.3
  42.5 0.0 copy-done
  42.6 60.2 %collective-permute-done = bf16[24,128,512]{2,1,0:T(8,128)(2,1)S(1)} collective-permute-done((bf16[24,128,512]{2,1,0:T(8,128)(2,1)}, bf16[24,128,512]{2,1,0:T(8,128)(2,1)S(1)}, u32[]{:S(2)}, u32[]{:S(2)}) %collective-permute-start) | collective-permute-done | bytes 3145760 | tf_op jit(solution)/shard_map/ppermute | solution.py:18
  102.8 0.4 fusion.50
  103.2 68.7 %collective-permute-done.1 = bf16[24,128,512]{2,1,0:T(8,128)(2,1)} collective-permute-done((bf16[24,128,512]{2,1,0:T(8,128)(2,1)}, bf16[24,128,512]{2,1,0:T(8,128)(2,1)}, u32[]{:S(2)}, u32[]{:S(2)}) %collective-permute-start.1) | collective-permute-done | bytes 3145760 | tf_op jit(solution)/shard_map/ppermute | solution.py:18
  171.9 2.1 fusion.51
  174.0 63.6 %collective-permute-done.2 = bf16[24,128,512]{2,1,0:T(8,128)(2,1)} collective-permute-done((bf16[24,128,512]{2,1,0:T(8,128)(2,1)}, bf16[24,128,512]{2,1,0:T(8,128)(2,1)}, u32[]{:S(2)}, u32[]{:S(2)}) %collective-permute-start.2) | collective-permute-done | bytes 3145760 | tf_op jit(solution)/shard_map/ppermute | solution.py:18
  237.6 2.1 fusion.52
  239.7 36.0 %collective-permute-done.3 = bf16[24,128,512]{2,1,0:T(8,128)(2,1)} collective-permute-done((bf16[24,128,512]{2,1,0:T(8,128)(2,1)}, bf16[24,128,512]{2,1,0:T(8,128)(2,1)}, u32[]{:S(2)}, u32[]{:S(2)}) %collective-permute-start.3) | collective-permute-done | bytes 3145760 | tf_op jit(solution)/shard_map/ppermute | solution.py:18
  275.7 2.1 fusion.53
  277.8 8.5 %fusion = (f32[128,512]{1,0:T(8,128)S(1)}, f32[128,512]{1,0:T(8,128)S(1)}, f32[128,512]{1,0:T(8,128)S(1)}, f32[128,512]{1,0:T(8,128)S(1)}, f32[128,512]{1,0:T(8,...) fusion(bf16[24,128,512]{2,1,0:T(8,128)(2,1)S(1)} %collective-permute-done, ...), kind=kLoop, calls=%fused_computation.16 | loop fusion | flops 63963136 | bytes 30408704 | tf_op jit(solution)/shard_map/wcf,wcf->cf/dot_general | solution.py:59
  286.5 1.4 multiply_add_fusion
  287.9 0.0 all-gather.2.cloned.1.call-update
  287.9 0.5 fusion.40
  288.4 94.1 %all-gather.2.cloned.1.call-done = f32[8,4,128,512]{3,2,1,0:T(8,128)} async-done(((f32[1,4,128,512]{3,2,1,0:T(8,128)}), f32[8,4,128,512]{3,2,1,0:T(8,128)}) %all-gather.2.cloned.1.call-update) | async-done | bytes 8388624 | tf_op jit(solution)/shard_map/all_gather | solution.py:87
  382.5 4.5 %reduce_sum.19 = f32[4,128,512]{2,1,0:T(8,128)S(1)} reduce(f32[8,4,128,512]{3,2,1,0:T(8,128)} %all-gather.2.cloned.1.call-done, f32[]{:T(128)} %constant.53.clone.1), dimensions={0}, to_apply=%region_1.2 | reduce | flops 1835008 | bytes 9437188 | tf_op jit(solution)/shard_map/reduce_sum | solution.py:87
  387.1 1.1 convolution_bitcast_fusion
  388.2 0.7 copy.5
  (12 shorter events, 0.2 us)
Async XLA Ops:
  6.5 376.0 %all-gather.2.cloned.1.call-start = ((), (), s32[]{:S(2)}) async-start(), calls=%async_computation | async-start | bytes 9437184 | tf_op jit(solution)/shard_map/all_gather | solution.py:87
  26.9 15.7 %copy-start = (s32[1,4]{1,0:T(1,128)S(1)}, s32[1,4]{1,0:T(1,128)}, u32[]{:S(2)}) copy-start(s32[1,4]{1,0:T(1,128)} %param.5) | copy-start | bytes 52
  31.9 70.9 %collective-permute-start = (bf16[24,128,512]{2,1,0:T(8,128)(2,1)}, bf16[24,128,512]{2,1,0:T(8,128)(2,1)S(1)}, u32[]{:S(2)}, u32[]{:S(2)}) collective-permute-start(bf16[24,128,512]{2,1,0:T(8,128)(2,1)} %fusion.8), channel_id=1, source_target_pairs={{8,0},{16,8},{24,16},{32,24},{40,32},{48,40},{56,48},{64,56},{72,6... | collective-permute-start | bytes 9437192 | tf_op jit(solution)/shard_map/ppermute | solution.py:18
  36.0 135.9 %collective-permute-start.1 = (bf16[24,128,512]{2,1,0:T(8,128)(2,1)}, bf16[24,128,512]{2,1,0:T(8,128)(2,1)}, u32[]{:S(2)}, u32[]{:S(2)}) collective-permute-start(bf16[24,128,512]{2,1,0:T(8,128)(2,1)} %fusion.8), channel_id=1, source_target_pairs={{16,0},{24,8},{32,16},{40,24},{48,32},{56,40},{64,48},{72,56},{80,... | collective-permute-start | bytes 9437192 | tf_op jit(solution)/shard_map/ppermute | solution.py:18
  38.5 199.1 %collective-permute-start.2 = (bf16[24,128,512]{2,1,0:T(8,128)(2,1)}, bf16[24,128,512]{2,1,0:T(8,128)(2,1)}, u32[]{:S(2)}, u32[]{:S(2)}) collective-permute-start(bf16[24,128,512]{2,1,0:T(8,128)(2,1)} %fusion.8), channel_id=1, source_target_pairs={{24,0},{32,8},{40,16},{48,24},{56,32},{64,40},{72,48},{80,56},{88,... | collective-permute-start | bytes 9437192 | tf_op jit(solution)/shard_map/ppermute | solution.py:18
  40.4 235.3 %collective-permute-start.3 = (bf16[24,128,512]{2,1,0:T(8,128)(2,1)}, bf16[24,128,512]{2,1,0:T(8,128)(2,1)}, u32[]{:S(2)}, u32[]{:S(2)}) collective-permute-start(bf16[24,128,512]{2,1,0:T(8,128)(2,1)} %fusion.8), channel_id=1, source_target_pairs={{32,0},{40,8},{48,16},{56,24},{64,32},{72,40},{80,48},{88,56},{96,... | collective-permute-start | bytes 9437192 | tf_op jit(solution)/shard_map/ppermute | solution.py:18
Sparse Core Ops, SparseCore 0:
  288.0 94.4 all-gather.1
